TPU v7x, 32 devices: a whole 2x2x4 slice. The times are simulated.
32 devices in a mesh: ctx: 8 (over z, y), wsh: 4 (over x, core).
Axes of the slice: x: 2, y: 2, z: 4, core: 2. Of those that a mesh axis runs over, the one named last changes fastest.
Arguments:
- tokens: bfloat16 [4, 1024, 2048], P('wsh', 'ctx'), may hold values from -6 to 6
- out_grad: bfloat16 [4, 1024, 2048], P('wsh', 'ctx'), may hold values from -6 to 6
- attn_weight: bfloat16 [4, 2048, 2048], P(None, None, 'wsh'), may hold values from -0.125 to 0.125
- mlp_weight: bfloat16 [3, 2048, 8192], P(None, None, 'wsh'), may hold values from -0.125 to 0.125
- norm_gains: bfloat16 [4, 2048], P(None, 'wsh'), may hold values from 0.25 to 1.75
- adapt_model: bfloat16 [11, 64, 2048], P(None, None, 'wsh'), may hold values from -0.125 to 0.125
- adapt_hidden: bfloat16 [3, 64, 8192], P(None, None, 'wsh'), may hold values from -0.0625 to 0.0625
- lengths: int32 [4], replicated, may hold values from 512 to 1024, as said below
- adapter_pick: int32 [4], replicated, may hold values from 0 to 3
- block_order: int32 [4, 16], P('wsh'), may hold values from 0 to 15, as said below
Outputs:
- layer_out: bfloat16 [4, 1024, 2048], P('wsh', 'ctx')
- input_grad: float32 [4, 1024, 2048], P('wsh', 'ctx')
- adapt_model_grad: float32 [11, 64, 2048], P(None, None, 'wsh')
- adapt_hidden_grad: float32 [3, 64, 8192], P(None, None, 'wsh')
Inputs may be any that keep to these rules, and one draw needn't show every extreme that they name: `lengths`: some sequence has exactly 1024 valid tokens. Each row of block_order is a permutation of the 16 blocks; the two blocks stored on one index of ctx are p and 15 - p for some p, in either order.
All inputs are finite; a program needn't handle non-finite values.
Results may differ from a plain program's by a relative error of at most 0.017.
Values may be sent and summed in bfloat16 or wider, within the bound.
No kernel may reach another device: no remote copies, remote signals or barrier semaphores. Data moves between devices by JAX's collectives and lax.ppermute only.
A program may use at most 512 MiB of HBM per device.

v0:
```python
import jax
import jax.numpy as jnp
from jax import lax
from jax.sharding import PartitionSpec as P

HEADS = 16
HEAD_DIM = 128
FF = 8192
RANK = 16
ADAPTERS = 4
NORM_EPS = 1e-06
ADAPTER_SCALE = 4.0
ROPE_BASE = 500000.0


def rms_scale(values):
    return lax.rsqrt(jnp.mean(values * values, axis=-1, keepdims=True) + NORM_EPS)


def norm_back(values, scale_rows, upstream):
    return scale_rows * upstream - values * scale_rows**3 * jnp.mean(
        upstream * values, axis=-1, keepdims=True
    )


def rotary_tables(positions, head_dim):
    half_dim = head_dim // 2
    frequency = ROPE_BASE ** (-(jnp.arange(half_dim, dtype=jnp.float32) * 2.0) / head_dim)
    angles = positions.astype(jnp.float32)[:, None] * frequency[None, :]
    return (jnp.cos(angles)[:, None, :], jnp.sin(angles)[:, None, :])


def rotate(values, tables, heads_total):
    cosine, sine_part = tables
    row_count = values.shape[0]
    shaped = values.reshape(row_count, heads_total, -1)
    half_dim = shaped.shape[-1] // 2
    first_half = shaped[..., :half_dim]
    second_half = shaped[..., half_dim:]
    turned = jnp.concatenate(
        [
            first_half * cosine - second_half * sine_part,
            second_half * cosine + first_half * sine_part,
        ],
        axis=-1,
    )
    return turned.reshape(row_count, -1)


def rotate_back(gradient, tables, heads_total):
    cosine, sine_part = tables
    row_count = gradient.shape[0]
    shaped = gradient.reshape(row_count, heads_total, -1)
    half_dim = shaped.shape[-1] // 2
    first_half = shaped[..., :half_dim]
    second_half = shaped[..., half_dim:]
    turned = jnp.concatenate(
        [
            first_half * cosine + second_half * sine_part,
            second_half * cosine - first_half * sine_part,
        ],
        axis=-1,
    )
    return turned.reshape(row_count, -1)


def pick_rows(stacked, onehot, adapters):
    part_count, col_count = (stacked.shape[0], stacked.shape[2])
    split_view = stacked.reshape(part_count, adapters, -1, col_count)
    return jnp.einsum(
        "kard,a->krd", split_view, onehot.astype(stacked.dtype), preferred_element_type=jnp.float32
    ).astype(stacked.dtype)


def per_device(
    tokens,
    out_grad,
    attn_weight,
    mlp_weight,
    norm_gains,
    adapt_model,
    adapt_hidden,
    lengths,
    adapter_pick,
    block_order,
):
    input_rows = tokens[0]
    row_count, model_dim = input_rows.shape
    block_rows = row_count // 2
    ctx_size = lax.axis_size("ctx")
    slot_rows = row_count * ctx_size
    heads_all = HEADS
    head_dim = HEAD_DIM
    adapters = ADAPTERS
    score_scale = head_dim ** (-0.5)
    seq_index = lax.axis_index("wsh")
    ctx_index = lax.axis_index("ctx")
    seq_length = lax.dynamic_index_in_dim(lengths, seq_index, keepdims=False)
    chosen = lax.dynamic_index_in_dim(adapter_pick, seq_index, keepdims=False)
    onehot = (jnp.arange(adapters) == chosen).astype(jnp.float32)
    all_positions = (
        block_order[0][:, None] * block_rows + jnp.arange(block_rows)[None, :]
    ).reshape(-1)
    own_positions = lax.dynamic_slice_in_dim(all_positions, ctx_index * row_count, row_count)
    valid_rows = (own_positions < seq_length).astype(jnp.float32)[:, None]
    tables = rotary_tables(own_positions, head_dim)
    key_allowed = (all_positions[None, :] <= own_positions[:, None]) & (
        all_positions[None, :] < seq_length
    )

    def heads_view(matrix):
        return matrix.reshape(matrix.shape[0], heads_all, head_dim)

    attn_full, gains_full, adapt_full = (
        lax.all_gather(attn_weight, "wsh", axis=2, tiled=True),
        lax.all_gather(norm_gains, "wsh", axis=1, tiled=True),
        lax.all_gather(adapt_model, "wsh", axis=2, tiled=True),
    )
    gain_rows = gains_full.astype(jnp.float32)
    model_reduced = pick_rows(adapt_full, onehot, adapters)
    projected_rows = jnp.einsum(
        "td,kde->kte", input_rows, attn_full[:3], preferred_element_type=jnp.float32
    )
    low_in = jnp.einsum(
        "td,krd->ktr", input_rows, model_reduced[:3], preferred_element_type=jnp.float32
    ).astype(jnp.bfloat16)
    projected_rows = projected_rows + ADAPTER_SCALE * jnp.einsum(
        "ktr,krd->ktd", low_in, model_reduced[6:9], preferred_element_type=jnp.float32
    )
    query_scale = rms_scale(projected_rows[0])
    key_scale = rms_scale(projected_rows[1])
    queries = rotate(projected_rows[0] * query_scale * gain_rows[0], tables, heads_all).astype(
        jnp.bfloat16
    )
    own_keys = rotate(projected_rows[1] * key_scale * gain_rows[1], tables, heads_all).astype(
        jnp.bfloat16
    )
    own_values = projected_rows[2].astype(jnp.bfloat16)
    all_keys, all_values = (
        lax.all_gather(own_keys, "ctx", axis=0, tiled=True),
        lax.all_gather(own_values, "ctx", axis=0, tiled=True),
    )
    query_heads = heads_view(queries)
    key_heads = heads_view(all_keys)
    value_heads = heads_view(all_values)
    scores = (
        jnp.einsum("thd,shd->hts", query_heads, key_heads, preferred_element_type=jnp.float32)
        * score_scale
    )
    scores = jnp.where(key_allowed[None], scores, -jnp.inf)
    row_max = jnp.max(scores, axis=-1, keepdims=True)
    log_full = row_max + jnp.log(jnp.sum(jnp.exp(scores - row_max), axis=-1, keepdims=True))
    weights = jnp.exp(scores - log_full).astype(jnp.bfloat16)
    attended = (
        jnp.einsum("hts,shd->thd", weights, value_heads, preferred_element_type=jnp.float32)
        .reshape(row_count, model_dim)
        .astype(jnp.bfloat16)
    )
    log_totals = log_full[..., 0]
    reduced_output = jnp.einsum(
        "td,rd->tr", attended, model_reduced[3], preferred_element_type=jnp.float32
    ).astype(jnp.bfloat16)
    branch = jnp.dot(
        attended, attn_full[3], preferred_element_type=jnp.float32
    ) + ADAPTER_SCALE * jnp.dot(
        reduced_output, model_reduced[9], preferred_element_type=jnp.float32
    )
    branch_scale = rms_scale(branch)
    hidden_in = input_rows.astype(jnp.float32) + branch * branch_scale * gain_rows[2]
    hidden_low = hidden_in.astype(jnp.bfloat16)
    reduced_gate_up = jnp.einsum(
        "td,krd->ktr", hidden_low, model_reduced[4:6], preferred_element_type=jnp.float32
    ).astype(jnp.bfloat16)

    def gate_up_parts(weight_piece, gathered_rows):
        gate_part = jnp.dot(
            hidden_low, weight_piece[0], preferred_element_type=jnp.float32
        ) + ADAPTER_SCALE * jnp.dot(
            reduced_gate_up[0], gathered_rows[0], preferred_element_type=jnp.float32
        )
        up_part = jnp.dot(
            hidden_low, weight_piece[1], preferred_element_type=jnp.float32
        ) + ADAPTER_SCALE * jnp.dot(
            reduced_gate_up[1], gathered_rows[1], preferred_element_type=jnp.float32
        )
        return (gate_part, up_part)

    weight_piece = lax.all_gather(mlp_weight, "wsh", axis=2, tiled=True)
    adapt_piece = lax.all_gather(adapt_hidden, "wsh", axis=2, tiled=True)
    gathered_rows = pick_rows(adapt_piece, onehot, adapters)
    gate_part, up_part = gate_up_parts(weight_piece, gathered_rows)
    product = (jax.nn.silu(gate_part) * up_part).astype(jnp.bfloat16)
    down_total_sum = jnp.einsum(
        "tn,dn->td", product, weight_piece[2], preferred_element_type=jnp.float32
    )
    low_down_sum = jnp.einsum(
        "tn,rn->tr", product, gathered_rows[2], preferred_element_type=jnp.float32
    )
    down_total_sum, low_down_sum = (down_total_sum, low_down_sum)
    low_down = low_down_sum.astype(jnp.bfloat16)
    feedforward_output = down_total_sum + ADAPTER_SCALE * jnp.dot(
        low_down, model_reduced[10], preferred_element_type=jnp.float32
    )
    mlp_scale = rms_scale(feedforward_output)
    result = hidden_in + feedforward_output * mlp_scale * gain_rows[3]
    upstream = out_grad[0].astype(jnp.float32) * valid_rows
    grad_mlp_out = norm_back(feedforward_output, mlp_scale, upstream * gain_rows[3]).astype(
        jnp.bfloat16
    )
    grad_low_down = (
        ADAPTER_SCALE
        * jnp.einsum(
            "td,rd->tr", grad_mlp_out, model_reduced[10], preferred_element_type=jnp.float32
        )
    ).astype(jnp.bfloat16)
    gradient_down_factor = ADAPTER_SCALE * jnp.einsum(
        "tr,td->rd", low_down, grad_mlp_out, preferred_element_type=jnp.float32
    )
    weight_piece = lax.all_gather(mlp_weight, "wsh", axis=2, tiled=True)
    adapt_piece = lax.all_gather(adapt_hidden, "wsh", axis=2, tiled=True)
    gathered_rows = pick_rows(adapt_piece, onehot, adapters)
    gate_part, up_part = gate_up_parts(weight_piece, gathered_rows)
    sigmoid_gate = jax.nn.sigmoid(gate_part)
    silu_gate = gate_part * sigmoid_gate
    product = (silu_gate * up_part).astype(jnp.bfloat16)
    grad_product = jnp.dot(
        grad_mlp_out, weight_piece[2], preferred_element_type=jnp.float32
    ) + jnp.dot(grad_low_down, gathered_rows[2], preferred_element_type=jnp.float32)
    grad_gate = (
        grad_product * up_part * sigmoid_gate * (1.0 + gate_part * (1.0 - sigmoid_gate))
    ).astype(jnp.bfloat16)
    grad_up = (grad_product * silu_gate).astype(jnp.bfloat16)
    input_sum = jnp.einsum(
        "tn,dn->td", grad_gate, weight_piece[0], preferred_element_type=jnp.float32
    ) + jnp.einsum("tn,dn->td", grad_up, weight_piece[1], preferred_element_type=jnp.float32)
    reduced_sum = ADAPTER_SCALE * jnp.stack(
        [
            jnp.einsum(
                "tn,rn->tr", grad_gate, gathered_rows[0], preferred_element_type=jnp.float32
            ),
            jnp.einsum("tn,rn->tr", grad_up, gathered_rows[1], preferred_element_type=jnp.float32),
        ]
    )
    piece_grads = jnp.stack(
        [
            ADAPTER_SCALE
            * jnp.einsum(
                "tr,tn->rn", reduced_gate_up[0], grad_gate, preferred_element_type=jnp.float32
            ),
            ADAPTER_SCALE
            * jnp.einsum(
                "tr,tn->rn", reduced_gate_up[1], grad_up, preferred_element_type=jnp.float32
            ),
            jnp.einsum("tr,tn->rn", grad_low_down, product, preferred_element_type=jnp.float32),
        ]
    )
    input_sum, reduced_sum, picked_hidden = (input_sum, reduced_sum, piece_grads)
    low_grads = reduced_sum.astype(jnp.bfloat16)
    grad_hidden = (
        upstream
        + input_sum
        + jnp.einsum(
            "ktr,krd->td", low_grads, model_reduced[4:6], preferred_element_type=jnp.float32
        )
    )
    grad_a_gate_up = jnp.einsum(
        "ktr,td->krd", low_grads, hidden_low, preferred_element_type=jnp.float32
    )
    grad_branch = norm_back(branch, branch_scale, grad_hidden * gain_rows[2]).astype(jnp.bfloat16)
    grad_low_out = (
        ADAPTER_SCALE
        * jnp.einsum("td,rd->tr", grad_branch, model_reduced[9], preferred_element_type=jnp.float32)
    ).astype(jnp.bfloat16)
    gradient_output_factor = ADAPTER_SCALE * jnp.einsum(
        "tr,td->rd", reduced_output, grad_branch, preferred_element_type=jnp.float32
    )
    grad_a_out = jnp.einsum("tr,td->rd", grad_low_out, attended, preferred_element_type=jnp.float32)
    grad_attended = (
        jnp.einsum("te,de->td", grad_branch, attn_full[3], preferred_element_type=jnp.float32)
        + jnp.einsum(
            "tr,rd->td", grad_low_out, model_reduced[3], preferred_element_type=jnp.float32
        )
    ).astype(jnp.bfloat16)
    grad_heads = heads_view(grad_attended)
    scores = (
        jnp.einsum("thd,shd->hts", query_heads, key_heads, preferred_element_type=jnp.float32)
        * score_scale
    )
    scores = jnp.where(key_allowed[None], scores, -jnp.inf)
    weights_full = jnp.exp(scores - log_totals[..., None])
    grad_probs = jnp.einsum(
        "thd,shd->hts", grad_heads, value_heads, preferred_element_type=jnp.float32
    )
    row_delta = jnp.sum(weights_full * grad_probs, axis=-1, keepdims=True)
    grad_scores = (weights_full * (grad_probs - row_delta)).astype(jnp.bfloat16)
    grad_queries = (
        jnp.einsum("hts,shd->thd", grad_scores, key_heads, preferred_element_type=jnp.float32)
        * score_scale
    ).reshape(row_count, model_dim)
    key_full = (
        jnp.einsum("hts,thd->shd", grad_scores, query_heads, preferred_element_type=jnp.float32)
        * score_scale
    ).reshape(slot_rows, model_dim)
    value_full = jnp.einsum(
        "hts,thd->shd",
        weights_full.astype(jnp.bfloat16),
        grad_heads,
        preferred_element_type=jnp.float32,
    ).reshape(slot_rows, model_dim)
    grad_keys, grad_values = (
        lax.psum_scatter(key_full, "ctx", scatter_dimension=0, tiled=True),
        lax.psum_scatter(value_full, "ctx", scatter_dimension=0, tiled=True),
    )
    grad_proj_query = norm_back(
        projected_rows[0], query_scale, rotate_back(grad_queries, tables, heads_all) * gain_rows[0]
    ).astype(jnp.bfloat16)
    grad_proj_key = norm_back(
        projected_rows[1], key_scale, rotate_back(grad_keys, tables, heads_all) * gain_rows[1]
    ).astype(jnp.bfloat16)
    grad_proj = jnp.stack([grad_proj_query, grad_proj_key, grad_values.astype(jnp.bfloat16)])
    grad_low_qkv = (
        ADAPTER_SCALE
        * jnp.einsum(
            "ktd,krd->ktr", grad_proj, model_reduced[6:9], preferred_element_type=jnp.float32
        )
    ).astype(jnp.bfloat16)
    gradient_projection_factor = ADAPTER_SCALE * jnp.einsum(
        "ktr,ktd->krd", low_in, grad_proj, preferred_element_type=jnp.float32
    )
    grad_a_qkv = jnp.einsum(
        "ktr,td->krd", grad_low_qkv, input_rows, preferred_element_type=jnp.float32
    )
    grad_inputs = (
        grad_hidden
        + jnp.einsum("kte,kde->td", grad_proj, attn_full[:3], preferred_element_type=jnp.float32)
        + jnp.einsum(
            "ktr,krd->td", grad_low_qkv, model_reduced[:3], preferred_element_type=jnp.float32
        )
    )
    picked_model = jnp.concatenate(
        [
            grad_a_qkv,
            grad_a_out[None],
            grad_a_gate_up,
            gradient_projection_factor,
            gradient_output_factor[None],
            gradient_down_factor[None],
        ],
        axis=0,
    )
    spread_model = (onehot[None, :, None, None] * picked_model[:, None]).reshape(
        picked_model.shape[0], adapters * RANK, model_dim
    )
    spread_hidden = (onehot[None, :, None, None] * picked_hidden[:, None]).reshape(
        picked_hidden.shape[0], adapters * RANK, FF
    )
    shard_model, shard_hidden = (
        lax.psum_scatter(spread_model, "wsh", scatter_dimension=2, tiled=True),
        lax.psum_scatter(spread_hidden, "wsh", scatter_dimension=2, tiled=True),
    )
    model_grads, hidden_grads_out = lax.psum((shard_model, shard_hidden), "ctx")
    return (result.astype(jnp.bfloat16)[None], grad_inputs[None], model_grads, hidden_grads_out)


def solution(mesh):
    in_specs = (
        P("wsh", "ctx", None),
        P("wsh", "ctx", None),
        P(None, None, "wsh"),
        P(None, None, "wsh"),
        P(None, "wsh"),
        P(None, None, "wsh"),
        P(None, None, "wsh"),
        P(),
        P(),
        P("wsh", None),
    )
    out_specs = (
        P("wsh", "ctx", None),
        P("wsh", "ctx", None),
        P(None, None, "wsh"),
        P(None, None, "wsh"),
    )
    return jax.shard_map(
        per_device, mesh=mesh, in_specs=in_specs, out_specs=out_specs, check_vma=False
    )
```

profile of v0, /device:TPU:0, one launch (start us, length us, event | category | flops | bytes accessed | tf_op | source)
XLA Modules:
  0.0 1708.9 jit_solution(13489928325962978200)
XLA Ops:
  7.9 11.5 copy.32
  20.4 6.4 all_gather.26
  29.2 10.2 all-gather.10.cloned.1.call-done
  39.4 4.8 fusion.19
  45.8 196.8 %all-gather.8.cloned.1.call-done = bf16[4,2048,2048]{1,2,0:T(8,128)(2,1)} async-done(((bf16[4,2048,512]{1,2,0:T(8,128)(2,1)}), bf16[4,2048,2048]{1,2,0:T(8,128)(2,1)}) %all-gather.8.cloned.1.call-update) | async-done | bytes 33554448 | tf_op jit(solution)/shard_map/all_gather | solution.py:115
  242.6 11.9 fusion.74
  257.7 2.8 copy.34
  260.4 2.5 copy.35
  268.2 2.1 copy.36
  272.9 6.7 fusion.17
  281.4 67.9 %all-gather.12.cloned.1.call-done = bf16[1024,2048]{0,1:T(8,128)(2,1)} async-done(((bf16[128,2048]{0,1:T(8,128)(2,1)}), bf16[1024,2048]{0,1:T(8,128)(2,1)}) %all-gather.12.cloned.1.call-update) | async-done | bytes 4194320 | tf_op jit(solution)/shard_map/all_gather | solution.py:140
  349.3 4.3 fusion.14
  353.6 2.5 exponential_reduce_fusion
  356.9 67.7 %all-gather.18.cloned.1.call-done = bf16[1,1024,2048]{1,2,0:T(8,128)(2,1)} async-done(((bf16[1,128,2048]{1,2,0:T(8,128)(2,1)}), bf16[1,1024,2048]{1,2,0:T(8,128)(2,1)}) %all-gather.18.cloned.1.call-update) | async-done | bytes 4194320 | tf_op jit(solution)/shard_map/all_gather | solution.py:141
  424.6 7.2 convolution_convert_fusion
  432.0 9.3 fusion.13
  442.3 565.8 %all-gather.14.cloned.1.call-done = bf16[3,2048,8192]{2,1,0:T(8,128)(2,1)} async-done(((bf16[3,2048,2048]{2,1,0:T(8,128)(2,1)}), bf16[3,2048,8192]{2,1,0:T(8,128)(2,1)}) %all-gather.14.cloned.1.call-update) | async-done | bytes 100663312 | tf_op jit(solution)/shard_map/all_gather | solution.py:188
  1008.1 15.0 fusion.1
  1023.1 5.0 fusion.8
  1028.1 15.2 fusion.3
  1043.3 7.1 multiply_convert_fusion.3
  1052.2 15.8 fusion.5
  1070.0 15.2 fusion.4
  1085.2 7.1 multiply_convert_fusion.1
  1093.6 16.7 fusion
  1110.4 17.0 fusion.37
  1130.7 4.6 fusion.12
  1136.0 8.2 multiply_reduce_fusion
  1144.2 2.6 multiply_convert_fusion
  1146.8 4.7 broadcast_multiply_fusion
  1151.6 9.4 fusion.81
  1163.0 2.2 fusion.10
  1165.7 3.4 bitcast_multiply_fusion
  1169.1 4.8 fusion.45
  1173.9 125.7 %reduce-scatter.5.cloned.1.call-done = f32[128,2048]{0,1:T(8,128)} async-done(((f32[1024,2048]{0,1:T(8,128)}), f32[128,2048]{0,1:T(8,128)}) %reduce-scatter.5.cloned.1.call-update) | async-done | bytes 1048592 | tf_op jit(solution)/shard_map/reduce_scatter | solution.py:311
  1299.6 2.1 fusion.98
  1306.7 2.7 copy.41
  1309.4 3.0 pad_maximum_fusion.3
  1312.4 2.5 copy.46
  1316.9 133.3 %reduce-scatter.7.cloned.1.call-done = f32[128,2048]{0,1:T(8,128)} async-done(((f32[1024,2048]{0,1:T(8,128)}), f32[128,2048]{0,1:T(8,128)}) %reduce-scatter.7.cloned.1.call-update) | async-done | bytes 1048592 | tf_op jit(solution)/shard_map/reduce_scatter | solution.py:312
  1451.5 2.1 fusion.65
  1457.0 3.3 bitcast_multiply_fusion.1
  1460.4 49.5 %reduce-scatter.11.cloned.1.call-done = f32[3,64,2048]{2,1,0:T(8,128)} async-done(((f32[3,64,8192]{2,1,0:T(8,128)}), f32[3,64,2048]{2,1,0:T(8,128)}) %reduce-scatter.11.cloned.1.call-update) | async-done | bytes 1572880 | tf_op jit(solution)/shard_map/reduce_scatter | solution.py:359
  1509.8 57.0 %reduce-scatter.9.cloned.1.call-done = f32[11,64,512]{2,1,0:T(8,128)} async-done(((f32[11,64,2048]{2,1,0:T(8,128)}), f32[11,64,512]{2,1,0:T(8,128)}) %reduce-scatter.9.cloned.1.call-update) | async-done | bytes 1441808 | tf_op jit(solution)/shard_map/reduce_scatter | solution.py:358
  1568.1 11.3 fusion.32
  1579.4 117.3 %all-reduce.3.cloned.1.call-done = (f32[11,64,512]{2,1,0:T(8,128)}, f32[3,64,2048]{2,1,0:T(8,128)}) async-done(((f32[11,64,512]{2,1,0:T(8,128)}, f32[3,64,2048]{2,1,0:T(8,128)}), (f32[11,64,512]{2,1,0:T(8,128)}, f32[3,64,2048]{2,1,0:T(8,128)})) %all-reduce.3.cloned.1.call-update) | async-done | bytes 3014672 | tf_op jit(solution)/shard_map/psum | solution.py:361
  1696.7 2.6 copy.86
  1699.3 2.7 copy.87
  (214 shorter events, 44.5 us)
Async XLA Ops:
  7.2 32.2 %all-gather.10.cloned.1.call-start = ((), (), s32[]{:S(2)}) async-start(), calls=%async_computation.5 | async-start | bytes 3604480 | tf_op jit(solution)/shard_map/all_gather | solution.py:117
  7.9 234.7 %all-gather.8.cloned.1.call-start = ((), (), s32[]{:S(2)}) async-start(), calls=%async_computation.4 | async-start | bytes 41943040 | tf_op jit(solution)/shard_map/all_gather | solution.py:115
  19.5 7.4 copy-start.58
  19.5 8.8 copy-start.59
  19.5 253.4 %all-gather.16.cloned.1.call-start = ((), (), s32[]{:S(2)}) async-start(), calls=%async_computation.8 | async-start | bytes 3932160 | tf_op jit(solution)/shard_map/all_gather | solution.py:189
  20.2 329.1 %all-gather.12.cloned.1.call-start = ((), (), s32[]{:S(2)}) async-start(), calls=%async_computation.6 | async-start | bytes 4718592 | tf_op jit(solution)/shard_map/all_gather | solution.py:140
  26.9 236.9 %copy-start.42 = (f32[1,2048]{1,0:T(1,128)}, f32[1,2048]{1,0:T(1,128)S(1)}, u32[]{:S(2)}) copy-start(f32[1,2048]{1,0:T(1,128)S(1)} %get-tuple-element.38) | copy-start | bytes 24580
  26.9 238.3 %copy-start.44 = (f32[1,2048]{1,0:T(1,128)}, f32[1,2048]{1,0:T(1,128)S(1)}, u32[]{:S(2)}) copy-start(f32[1,2048]{1,0:T(1,128)S(1)} %get-tuple-element.39) | copy-start | bytes 24580
  29.1 236.3 %copy-start.32 = (f32[128,64]{1,0:T(8,128)}, f32[128,64]{1,0:T(8,128)S(1)}, u32[]{:S(2)}) copy-start(f32[128,64]{1,0:T(8,128)S(1)} %get-tuple-element.40) | copy-start | bytes 98308
  29.1 236.3 %copy-start.34 = (f32[128,64]{1,0:T(8,128)}, f32[128,64]{1,0:T(8,128)S(1)}, u32[]{:S(2)}) copy-start(f32[128,64]{1,0:T(8,128)S(1)} %get-tuple-element.41) | copy-start | bytes 98308
  39.4 6.1 copy-start.4
  45.8 208.7 %copy-start.46 = (bf16[3,16,128]{2,1,0:T(8,128)(2,1)}, bf16[3,16,128]{2,1,0:T(8,128)(2,1)S(1)}, u32[]{:S(2)}) copy-start(bf16[3,16,128]{2,1,0:T(8,128)(2,1)S(1)} %convolution_convert_fusion.1) | copy-start | bytes 36868
  256.1 14.3 copy-start.1
  270.3 154.3 %all-gather.18.cloned.1.call-start = ((), (), s32[]{:S(2)}) async-start(), calls=%async_computation.13 | async-start | bytes 4718592 | tf_op jit(solution)/shard_map/all_gather | solution.py:141
  271.3 736.9 %all-gather.14.cloned.1.call-start = ((), (), s32[]{:S(2)}) async-start(), calls=%async_computation.7 | async-start | bytes 125829120 | tf_op jit(solution)/shard_map/all_gather | solution.py:188
  271.8 1027.7 %reduce-scatter.5.cloned.1.call-start = ((), (), s32[]{:S(2)}) async-start(), calls=%async_computation.9 | async-start | bytes 9437184 | tf_op jit(solution)/shard_map/reduce_scatter | solution.py:311
  272.9 76.4 %copy-start.20 = (bf16[128,16,64]{2,0,1:T(8,128)(2,1)S(1)}, bf16[128,16,64]{2,0,1:T(8,128)(2,1)}, u32[]{:S(2)}) copy-start(bf16[128,16,64]{2,0,1:T(8,128)(2,1)} %get-tuple-element.24) | copy-start | bytes 786436
  272.9 76.4 %copy-start.22 = (bf16[128,16,64]{2,0,1:T(8,128)(2,1)S(1)}, bf16[128,16,64]{2,0,1:T(8,128)(2,1)}, u32[]{:S(2)}) copy-start(bf16[128,16,64]{2,0,1:T(8,128)(2,1)} %get-tuple-element.25) | copy-start | bytes 786436
  424.6 7.2 copy-start.13
  431.8 9.6 copy-start.28
  432.0 9.4 copy-start.48
  432.0 9.8 copy-start.5
  442.1 586.1 %copy-start.14 = (bf16[128,2048]{1,0:T(8,128)(2,1)}, bf16[128,2048]{1,0:T(8,128)(2,1)S(1)}, u32[]{:S(2)}) copy-start(bf16[128,2048]{1,0:T(8,128)(2,1)S(1)} %fusion.68) | copy-start | bytes 1572868
  1050.5 17.5 %copy-start.7 = (bf16[128,8192]{1,0:T(8,128)(2,1)}, bf16[128,8192]{1,0:T(8,128)(2,1)S(1)}, u32[]{:S(2)}) copy-start(bf16[128,8192]{1,0:T(8,128)(2,1)S(1)} %get-tuple-element.54) | copy-start | bytes 6291460
  1052.2 15.8 copy-start.30
  1085.2 7.1 copy-start.24
  1092.3 18.1 %copy-start.11 = (bf16[128,8192]{1,0:T(8,128)(2,1)}, bf16[128,8192]{1,0:T(8,128)(2,1)S(1)}, u32[]{:S(2)}) copy-start(bf16[128,8192]{1,0:T(8,128)(2,1)S(1)} %get-tuple-element.14) | copy-start | bytes 6291460
  1093.6 16.8 copy-start.31
  1130.4 4.9 copy-start.18
  1136.0 8.2 slice-start
  1136.0 8.2 slice-start.1
  1151.6 298.6 %reduce-scatter.7.cloned.1.call-start = ((), (), s32[]{:S(2)}) async-start(), calls=%async_computation.10 | async-start | bytes 9437184 | tf_op jit(solution)/shard_map/reduce_scatter | solution.py:312
  1161.0 348.8 %reduce-scatter.11.cloned.1.call-start = ((), (), s32[]{:S(2)}) async-start(), calls=%async_computation.12 | async-start | bytes 7864320 | tf_op jit(solution)/shard_map/reduce_scatter | solution.py:359
  1169.1 397.7 %reduce-scatter.9.cloned.1.call-start = ((), (), s32[]{:S(2)}) async-start(), calls=%async_computation.11 | async-start | bytes 7208960 | tf_op jit(solution)/shard_map/reduce_scatter | solution.py:358
  1173.9 129.5 %copy-start.33 = (f32[128,64]{1,0:T(8,128)S(1)}, f32[128,64]{1,0:T(8,128)}, u32[]{:S(2)}) copy-start(f32[128,64]{1,0:T(8,128)} %copy-done.32) | copy-start | bytes 98308
  1173.9 129.5 %copy-start.35 = (f32[128,64]{1,0:T(8,128)S(1)}, f32[128,64]{1,0:T(8,128)}, u32[]{:S(2)}) copy-start(f32[128,64]{1,0:T(8,128)} %copy-done.34) | copy-start | bytes 98308
  1306.7 8.2 copy-start.2
  1306.7 8.2 copy-start.43
  1306.7 8.2 copy-start.45
  1312.4 139.1 %copy-start.51 = (f32[128]{0:T(128)S(1)}, f32[128]{0:T(128)}, u32[]{:S(2)}) copy-start(f32[128]{0:T(128)} %copy-done.50) | copy-start | bytes 1540
  1312.4 139.1 %copy-start.53 = (f32[128]{0:T(128)S(1)}, f32[128]{0:T(128)}, u32[]{:S(2)}) copy-start(f32[128]{0:T(128)} %copy-done.52) | copy-start | bytes 1540
  1312.4 139.1 %copy-start.55 = (f32[128]{0:T(128)S(1)}, f32[128]{0:T(128)}, u32[]{:S(2)}) copy-start(f32[128]{0:T(128)} %get-tuple-element.44) | copy-start | bytes 1540
  1312.4 139.1 %copy-start.56 = (f32[128]{0:T(128)S(1)}, f32[128]{0:T(128)}, u32[]{:S(2)}) copy-start(f32[128]{0:T(128)} %get-tuple-element.62) | copy-start | bytes 1540
  1460.3 107.8 %copy-start.27 = (f32[128,2048]{1,0:T(8,128)S(1)}, f32[128,2048]{1,0:T(8,128)}, u32[]{:S(2)}) copy-start(f32[128,2048]{1,0:T(8,128)} %copy-done.26) | copy-start | bytes 3145732
  1460.3 107.8 %copy-start.37 = (bf16[1,128,2048]{1,2,0:T(8,128)(2,1)S(1)}, bf16[1,128,2048]{1,2,0:T(8,128)(2,1)}, u32[]{:S(2)}) copy-start(bf16[1,128,2048]{1,2,0:T(8,128)(2,1)} %copy-done.36) | copy-start | bytes 1572868
  1460.3 107.8 %copy-start.39 = (bf16[1,128,2048]{1,2,0:T(8,128)(2,1)S(1)}, bf16[1,128,2048]{1,2,0:T(8,128)(2,1)}, u32[]{:S(2)}) copy-start(bf16[1,128,2048]{1,2,0:T(8,128)(2,1)} %copy-done.38) | copy-start | bytes 1572868
  1460.3 107.8 %copy-start.41 = (bf16[1,128,2048]{1,2,0:T(8,128)(2,1)S(1)}, bf16[1,128,2048]{1,2,0:T(8,128)(2,1)}, u32[]{:S(2)}) copy-start(bf16[1,128,2048]{1,2,0:T(8,128)(2,1)} %copy-done.40) | copy-start | bytes 1572868
  1460.3 236.4 %all-reduce.3.cloned.1.call-start = ((), (), s32[]{:S(2)}) async-start(), calls=%async_computation.14 | async-start | bytes 6029312 | tf_op jit(solution)/shard_map/psum | solution.py:361
  (25 other events, 65.0 us)
Sparse Core Ops, SparseCore 0:
  9.5 29.8 all-gather.9
  41.0 201.5 all-gather.7
  244.1 28.4 all-gather.15
  274.6 74.6 all-gather.11
  351.8 72.8 all-gather.17
  426.0 582.0 all-gather.13
  1151.7 147.8 reduce-scatter.4
  1303.2 146.9 reduce-scatter.6
  1452.7 57.0 reduce-scatter.10
  1512.2 54.5 reduce-scatter.8
  1570.6 126.0 all-reduce.2
where the time goes:
time: 1720 us; the launch traced here: 1710 us
  waiting for transfers between devices  1390 us (81%)
  matrix products  217 us (13%)
  local copies, waits for them, and re-layouts  42.7 us (2%)
  other arithmetic  33.2 us (2%)
    all_gather x1, waiting for transfers between devices, per_device(): weight_piece = lax.all_gather(mlp_weight, 'wsh', axis=2, tiled=True)  566 us
    all_gather x1, waiting for transfers between devices, per_device(): lax.all_gather(attn_weight, 'wsh', axis=2, tiled=True)  197 us
    reduce_scatter x1, waiting for transfers between devices, per_device(): lax.psum_scatter(value_full, 'ctx', scatter_dimension=0, tiled=True)  133 us
    reduce_scatter x1, waiting for transfers between devices, per_device(): lax.psum_scatter(key_full, 'ctx', scatter_dimension=0, tiled=True)  126 us
    psum x1, waiting for transfers between devices, per_device(): model_grads, hidden_grads_out = lax.psum((shard_model, shard_hidden), 'ctx')  117 us
    all_gather x1, waiting for transfers between devices, per_device(): lax.all_gather(own_keys, 'ctx', axis=0, tiled=True)  67.9 us
    all_gather x1, waiting for transfers between devices, per_device(): lax.all_gather(own_values, 'ctx', axis=0, tiled=True)  67.7 us
    reduce_scatter x1, waiting for transfers between devices, per_device(): lax.psum_scatter(spread_model, 'wsh', scatter_dimension=2, tiled=True)  57 us
  transfers between devices with their start and end apart: 11, of which 10 were waited for; matrix products, arithmetic and copies ran while one was open for 8% of the time, Pallas kernels for 0%

commit v1 on v0

--- a/solution.py
+++ b/solution.py
@@ -185,7 +185,14 @@
         )
         return (gate_part, up_part)
 
-    weight_piece = lax.all_gather(mlp_weight, "wsh", axis=2, tiled=True)
+    x = mlp_weight
+    ways, here, hop = (lax.axis_size("wsh"), lax.axis_index("wsh"), x.shape[2])
+    shape = [n * ways if d == 2 else n for d, n in enumerate(x.shape)]
+    full = lax.dynamic_update_slice_in_dim(jnp.zeros(shape, x.dtype), x, here * hop, axis=2)
+    for far in range(1, ways):
+        x = lax.ppermute(x, "wsh", [(d, (d + 1) % ways) for d in range(ways)])
+        full = lax.dynamic_update_slice_in_dim(full, x, (here - far) % ways * hop, axis=2)
+    weight_piece = full
     adapt_piece = lax.all_gather(adapt_hidden, "wsh", axis=2, tiled=True)
     gathered_rows = pick_rows(adapt_piece, onehot, adapters)
     gate_part, up_part = gate_up_parts(weight_piece, gathered_rows)

time: 1720 us -> 2390 us (1.39)
  waiting for transfers between devices: 1390 us -> 1900 us
  local copies, waits for them, and re-layouts: 42.7 us -> 167 us
  matrix products: 217 us -> 248 us
    ppermute x0 -> x3, waiting for transfers between devices: none -> 1210 us  [per_device(): x = lax.ppermute(x, 'wsh', [(d, (d + 1) % ways) for d in range(ways)])]
    all_gather x1, waiting for transfers between devices: 566 us -> 0.01 us  [per_device(): weight_piece = lax.all_gather(mlp_weight, 'wsh', axis=2, tiled=True)]
    dynamic_update_slice x0 -> x4, local copies, waits for them, and re-layouts: none -> 83.9 us  [the longest x3 62.9 us: per_device(): lax.dynamic_update_slice_in_dim(full, x, (here - far) % ways * hop, axis=2)]
    all_gather x1, waiting for transfers between devices: 67.9 us -> 0.01 us  [per_device(): lax.all_gather(own_keys, 'ctx', axis=0, tiled=True)]
    all_gather x1, waiting for transfers between devices: 67.7 us -> 0.02 us  [per_device(): lax.all_gather(own_values, 'ctx', axis=0, tiled=True)]
    broadcast_in_dim x0 -> x1, local copies, waits for them, and re-layouts: none -> 31 us  [per_device(): jnp.zeros(shape, x.dtype)]
  transfers between devices with their start and end apart: 11 -> 14, of which waited for: 10 -> 10; matrix products, arithmetic and copies ran while one was open for 8% -> 13% of each run, Pallas kernels for 0% -> 0%
where the time goes in v1:
time: 2390 us; the launch traced here: 2380 us
  waiting for transfers between devices  1900 us (79%)
  matrix products  248 us (10%)
  local copies, waits for them, and re-layouts  167 us (7%)
  other arithmetic  35.2 us (1%)
    ppermute x3, waiting for transfers between devices, per_device(): x = lax.ppermute(x, 'wsh', [(d, (d + 1) % ways) for d in range(ways)])  1210 us
    all_gather x1, waiting for transfers between devices, per_device(): lax.all_gather(attn_weight, 'wsh', axis=2, tiled=True)  197 us
    reduce_scatter x1, waiting for transfers between devices, per_device(): lax.psum_scatter(value_full, 'ctx', scatter_dimension=0, tiled=True)  133 us
    reduce_scatter x1, waiting for transfers between devices, per_device(): lax.psum_scatter(key_full, 'ctx', scatter_dimension=0, tiled=True)  123 us
    psum x1, waiting for transfers between devices, per_device(): model_grads, hidden_grads_out = lax.psum((shard_model, shard_hidden), 'ctx')  117 us
    dynamic_update_slice x3, local copies, waits for them, and re-layouts, per_device(): lax.dynamic_update_slice_in_dim(full, x, (here - far) % ways * hop, axis=2)  62.9 us
    reduce_scatter x1, waiting for transfers between devices, per_device(): lax.psum_scatter(spread_model, 'wsh', scatter_dimension=2, tiled=True)  56.9 us
    reduce_scatter x1, waiting for transfers between devices, per_device(): lax.psum_scatter(spread_hidden, 'wsh', scatter_dimension=2, tiled=True)  49.4 us
  transfers between devices with their start and end apart: 14, of which 10 were waited for; matrix products, arithmetic and copies ran while one was open for 13% of the time, Pallas kernels for 0%

profile of v1, /device:TPU:0, one launch (start us, length us, event | category | flops | bytes accessed | tf_op | source)
XLA Modules:
  0.0 2375.4 jit_solution(6121161852607560589)
XLA Ops:
  7.9 11.5 copy.32
  20.3 6.4 all_gather.25
  30.4 9.0 all-gather.10.cloned.1.call-done
  39.4 4.8 fusion.23
  45.8 196.8 %all-gather.8.cloned.1.call-done = bf16[4,2048,2048]{1,2,0:T(8,128)(2,1)} async-done(((bf16[4,2048,512]{1,2,0:T(8,128)(2,1)}), bf16[4,2048,2048]{1,2,0:T(8,128)(2,1)}) %all-gather.8.cloned.1.call-update) | async-done | bytes 33554448 | tf_op jit(solution)/shard_map/all_gather | solution.py:115
  242.6 11.9 fusion.79
  257.7 2.7 copy.35
  272.2 435.0 %collective-permute-done = bf16[3,2048,2048]{2,1,0:T(8,128)(2,1)S(1)} collective-permute-done((bf16[3,2048,2048]{2,1,0:T(8,128)(2,1)}, bf16[3,2048,2048]{2,1,0:T(8,128)(2,1)S(1)}, u32[]{:S(2)}, u32[]{:S(2)}) %collective-permute-start) | collective-permute-done | bytes 25165856 | tf_op jit(solution)/shard_map/ppermute | solution.py:193
  707.2 8.3 copy-done.4
  715.5 638.3 %collective-permute-done.1 = bf16[3,2048,2048]{2,1,0:T(8,128)(2,1)} collective-permute-done((bf16[3,2048,2048]{2,1,0:T(8,128)(2,1)S(1)}, bf16[3,2048,2048]{2,1,0:T(8,128)(2,1)}, u32[]{:S(2)}, u32[]{:S(2)}) %collective-permute-start.1) | collective-permute-done | bytes 25165856 | tf_op jit(solution)/shard_map/ppermute | solution.py:193
  1355.2 31.0 %broadcast_in_dim.30 = bf16[3,2048,8192]{2,1,0:T(8,128)(2,1)} broadcast(bf16[]{:T(256)} %constant.91.clone.1), dimensions={} | broadcast | bytes 100663296 | tf_op jit(solution)/shard_map/broadcast_in_dim | solution.py:191
  1386.2 21.0 constant_dynamic-update-slice_fusion.3
  1407.1 6.6 fusion.21
  1414.6 20.9 constant_dynamic-update-slice_fusion.2
  1435.6 21.0 constant_dynamic-update-slice_fusion.1
  1456.6 4.3 fusion.18
  1464.3 7.2 convolution_convert_fusion
  1471.7 6.4 fusion.17
  1480.1 2.8 convolution_multiply_fusion.1
  1483.0 2.7 convolution_multiply_fusion
  1485.6 141.6 %collective-permute-done.2 = bf16[3,2048,2048]{2,1,0:T(8,128)(2,1)} collective-permute-done((bf16[3,2048,2048]{2,1,0:T(8,128)(2,1)}, bf16[3,2048,2048]{2,1,0:T(8,128)(2,1)}, u32[]{:S(2)}, u32[]{:S(2)}) %collective-permute-start.2) | collective-permute-done | bytes 25165856 | tf_op jit(solution)/shard_map/ppermute | solution.py:193
  1627.2 20.9 constant_dynamic-update-slice_fusion
  1648.2 16.2 fusion.12
  1664.4 15.1 multiply_convert_fusion.4
  1681.8 19.3 fusion.59
  1703.1 15.0 fusion
  1718.1 4.9 convolution_add_fusion
  1723.1 16.2 fusion.11
  1739.2 18.7 multiply_convert_fusion.3
  1759.3 17.0 fusion.4
  1776.3 16.3 fusion.41
  1796.6 4.7 fusion.16
  1802.8 8.2 multiply_reduce_fusion
  1813.5 4.7 broadcast_multiply_fusion
  1818.3 9.4 fusion.86
  1831.4 3.5 convolution_bitcast_fusion
  1835.0 3.4 bitcast_multiply_fusion
  1838.4 4.8 fusion.49
  1843.2 123.0 %reduce-scatter.5.cloned.1.call-done = f32[128,2048]{0,1:T(8,128)} async-done(((f32[1024,2048]{0,1:T(8,128)}), f32[128,2048]{0,1:T(8,128)}) %reduce-scatter.5.cloned.1.call-update) | async-done | bytes 1048592 | tf_op jit(solution)/shard_map/reduce_scatter | solution.py:318
  1973.3 2.7 copy.46
  1976.0 3.0 pad_maximum_fusion.2
  1983.5 133.3 %reduce-scatter.7.cloned.1.call-done = f32[128,2048]{0,1:T(8,128)} async-done(((f32[1024,2048]{0,1:T(8,128)}), f32[128,2048]{0,1:T(8,128)}) %reduce-scatter.7.cloned.1.call-update) | async-done | bytes 1048592 | tf_op jit(solution)/shard_map/reduce_scatter | solution.py:319
  2123.7 3.3 bitcast_multiply_fusion.1
  2127.1 49.4 %reduce-scatter.11.cloned.1.call-done = f32[3,64,2048]{2,1,0:T(8,128)} async-done(((f32[3,64,8192]{2,1,0:T(8,128)}), f32[3,64,2048]{2,1,0:T(8,128)}) %reduce-scatter.11.cloned.1.call-update) | async-done | bytes 1572880 | tf_op jit(solution)/shard_map/reduce_scatter | solution.py:366
  2176.5 56.9 %reduce-scatter.9.cloned.1.call-done = f32[11,64,512]{2,1,0:T(8,128)} async-done(((f32[11,64,2048]{2,1,0:T(8,128)}), f32[11,64,512]{2,1,0:T(8,128)}) %reduce-scatter.9.cloned.1.call-update) | async-done | bytes 1441808 | tf_op jit(solution)/shard_map/reduce_scatter | solution.py:365
  2234.7 11.3 fusion.35
  2246.0 117.4 %all-reduce.3.cloned.1.call-done = (f32[11,64,512]{2,1,0:T(8,128)}, f32[3,64,2048]{2,1,0:T(8,128)}) async-done(((f32[11,64,512]{2,1,0:T(8,128)}, f32[3,64,2048]{2,1,0:T(8,128)}), (f32[11,64,512]{2,1,0:T(8,128)}, f32[3,64,2048]{2,1,0:T(8,128)})) %all-reduce.3.cloned.1.call-update) | async-done | bytes 3014672 | tf_op jit(solution)/shard_map/psum | solution.py:368
  2366.0 2.7 copy.91
  (257 shorter events, 68.6 us)
Async XLA Ops:
  7.2 32.2 %all-gather.10.cloned.1.call-start = ((), (), s32[]{:S(2)}) async-start(), calls=%async_computation.5 | async-start | bytes 3604480 | tf_op jit(solution)/shard_map/all_gather | solution.py:117
  7.9 234.7 %all-gather.8.cloned.1.call-start = ((), (), s32[]{:S(2)}) async-start(), calls=%async_computation.4 | async-start | bytes 41943040 | tf_op jit(solution)/shard_map/all_gather | solution.py:115
  19.5 9.9 copy-start.73
  19.5 1387.6 %all-gather.14.cloned.1.call-start = ((), (), s32[]{:S(2)}) async-start(), calls=%async_computation.7 | async-start | bytes 3932160 | tf_op jit(solution)/shard_map/all_gather | solution.py:196
  20.2 1436.4 %all-gather.12.cloned.1.call-start = ((), (), s32[]{:S(2)}) async-start(), calls=%async_computation.6 | async-start | bytes 4718592 | tf_op jit(solution)/shard_map/all_gather | solution.py:140
  27.3 236.5 %copy-start.47 = (f32[1,2048]{1,0:T(1,128)}, f32[1,2048]{1,0:T(1,128)S(1)}, u32[]{:S(2)}) copy-start(f32[1,2048]{1,0:T(1,128)S(1)} %get-tuple-element.39) | copy-start | bytes 24580
  27.3 237.9 %copy-start.45 = (f32[1,2048]{1,0:T(1,128)}, f32[1,2048]{1,0:T(1,128)S(1)}, u32[]{:S(2)}) copy-start(f32[1,2048]{1,0:T(1,128)S(1)} %get-tuple-element.38) | copy-start | bytes 24580
  27.3 1451.8 %copy-start.49 = (f32[1,2048]{1,0:T(1,128)}, f32[1,2048]{1,0:T(1,128)S(1)}, u32[]{:S(2)}) copy-start(f32[1,2048]{1,0:T(1,128)S(1)} %get-tuple-element.37) | copy-start | bytes 24580
  30.3 235.1 %copy-start.33 = (f32[128,64]{1,0:T(8,128)}, f32[128,64]{1,0:T(8,128)S(1)}, u32[]{:S(2)}) copy-start(f32[128,64]{1,0:T(8,128)S(1)} %get-tuple-element.40) | copy-start | bytes 98308
  30.3 235.1 %copy-start.35 = (f32[128,64]{1,0:T(8,128)}, f32[128,64]{1,0:T(8,128)S(1)}, u32[]{:S(2)}) copy-start(f32[128,64]{1,0:T(8,128)S(1)} %get-tuple-element.41) | copy-start | bytes 98308
  45.8 208.7 %copy-start.54 = (bf16[3,16,128]{2,1,0:T(8,128)(2,1)}, bf16[3,16,128]{2,1,0:T(8,128)(2,1)S(1)}, u32[]{:S(2)}) copy-start(bf16[3,16,128]{2,1,0:T(8,128)(2,1)S(1)} %convolution_convert_fusion.1) | copy-start | bytes 36868
  256.1 14.2 copy-start.1
  270.3 1194.0 %all-gather.18.cloned.1.call-start = ((), (), s32[]{:S(2)}) async-start(), calls=%async_computation.13 | async-start | bytes 4718592 | tf_op jit(solution)/shard_map/all_gather | solution.py:141
  271.2 1431.9 %all-gather.16.cloned.1.call-start = ((), (), s32[]{:S(2)}) async-start(), calls=%async_computation.8 | async-start | bytes 125829120 | tf_op jit(solution)/shard_map/all_gather | solution.py:226
  271.8 1694.4 %reduce-scatter.5.cloned.1.call-start = ((), (), s32[]{:S(2)}) async-start(), calls=%async_computation.9 | async-start | bytes 9437184 | tf_op jit(solution)/shard_map/reduce_scatter | solution.py:318
  271.9 435.3 %collective-permute-start = (bf16[3,2048,2048]{2,1,0:T(8,128)(2,1)}, bf16[3,2048,2048]{2,1,0:T(8,128)(2,1)S(1)}, u32[]{:S(2)}, u32[]{:S(2)}) collective-permute-start(bf16[3,2048,2048]{2,1,0:T(8,128)(2,1)} %param.13), channel_id=1, source_target_pairs={{0,1},{1,2},{2,3},{3,0},{4,5},{5,6},{6,7},{7,4},{8,9},{9,10},{10,1... | collective-permute-start | bytes 75497480 | tf_op jit(solution)/shard_map/ppermute | solution.py:193
  707.2 8.3 copy-start.4
  715.5 638.3 %collective-permute-start.1 = (bf16[3,2048,2048]{2,1,0:T(8,128)(2,1)S(1)}, bf16[3,2048,2048]{2,1,0:T(8,128)(2,1)}, u32[]{:S(2)}, u32[]{:S(2)}) collective-permute-start(bf16[3,2048,2048]{2,1,0:T(8,128)(2,1)S(1)} %collective-permute-done), channel_id=1, source_target_pairs={{0,1},{1,2},{2,3},{3,0},{4,5},{5,6},{6,7},{7,4},{8,9},{9,10},{10,1... | collective-permute-start | bytes 75497480 | tf_op jit(solution)/shard_map/ppermute | solution.py:193
  1353.8 273.4 %collective-permute-start.2 = (bf16[3,2048,2048]{2,1,0:T(8,128)(2,1)}, bf16[3,2048,2048]{2,1,0:T(8,128)(2,1)}, u32[]{:S(2)}, u32[]{:S(2)}) collective-permute-start(bf16[3,2048,2048]{2,1,0:T(8,128)(2,1)} %collective-permute-done.1), channel_id=1, source_target_pairs={{0,1},{1,2},{2,3},{3,0},{4,5},{5,6},{6,7},{7,4},{8,9},{9,10},{10,1... | collective-permute-start | bytes 75497480 | tf_op jit(solution)/shard_map/ppermute | solution.py:193
  1355.1 109.1 %copy-start.14 = (pred[128,1024]{1,0:T(8,128)(4,1)}, pred[128,1024]{1,0:T(8,128)(4,1)S(1)}, u32[]{:S(2)}) copy-start(pred[128,1024]{1,0:T(8,128)(4,1)S(1)} %compare_and_fusion) | copy-start | bytes 393220
  1435.5 21.0 copy-start.22
  1435.5 21.0 copy-start.24
  1479.8 259.4 %copy-start.16 = (bf16[128,2048]{1,0:T(8,128)(2,1)}, bf16[128,2048]{1,0:T(8,128)(2,1)S(1)}, u32[]{:S(2)}) copy-start(bf16[128,2048]{1,0:T(8,128)(2,1)S(1)} %fusion.73) | copy-start | bytes 1572868
  1664.4 17.4 copy-start.53
  1664.4 17.4 copy-start.67
  1681.5 19.6 copy-start.58
  1702.8 15.3 copy-start.18
  1776.3 16.4 copy-start.6
  1776.3 16.4 copy-start.50
  1776.3 17.7 copy-start.9
  1776.3 17.7 copy-start.27
  1776.3 17.8 copy-start.66
  1776.3 17.8 copy-start.70
  1802.7 8.2 slice-start
  1818.3 298.5 %reduce-scatter.7.cloned.1.call-start = ((), (), s32[]{:S(2)}) async-start(), calls=%async_computation.10 | async-start | bytes 9437184 | tf_op jit(solution)/shard_map/reduce_scatter | solution.py:319
  1827.8 348.7 %reduce-scatter.11.cloned.1.call-start = ((), (), s32[]{:S(2)}) async-start(), calls=%async_computation.12 | async-start | bytes 7864320 | tf_op jit(solution)/shard_map/reduce_scatter | solution.py:366
  1838.4 395.1 %reduce-scatter.9.cloned.1.call-start = ((), (), s32[]{:S(2)}) async-start(), calls=%async_computation.11 | async-start | bytes 7208960 | tf_op jit(solution)/shard_map/reduce_scatter | solution.py:365
  1843.2 126.8 %copy-start.34 = (f32[128,64]{1,0:T(8,128)S(1)}, f32[128,64]{1,0:T(8,128)}, u32[]{:S(2)}) copy-start(f32[128,64]{1,0:T(8,128)} %copy-done.33) | copy-start | bytes 98308
  1843.2 126.8 %copy-start.36 = (f32[128,64]{1,0:T(8,128)S(1)}, f32[128,64]{1,0:T(8,128)}, u32[]{:S(2)}) copy-start(f32[128,64]{1,0:T(8,128)} %copy-done.35) | copy-start | bytes 98308
  1979.0 139.1 %copy-start.61 = (f32[128]{0:T(128)S(1)}, f32[128]{0:T(128)}, u32[]{:S(2)}) copy-start(f32[128]{0:T(128)} %copy-done.60) | copy-start | bytes 1540
  1979.0 139.1 %copy-start.63 = (f32[128]{0:T(128)S(1)}, f32[128]{0:T(128)}, u32[]{:S(2)}) copy-start(f32[128]{0:T(128)} %copy-done.62) | copy-start | bytes 1540
  1979.0 139.1 %copy-start.68 = (f32[128]{0:T(128)S(1)}, f32[128]{0:T(128)}, u32[]{:S(2)}) copy-start(f32[128]{0:T(128)} %get-tuple-element.44) | copy-start | bytes 1540
  1979.0 139.1 %copy-start.69 = (f32[128]{0:T(128)S(1)}, f32[128]{0:T(128)}, u32[]{:S(2)}) copy-start(f32[128]{0:T(128)} %get-tuple-element.61) | copy-start | bytes 1540
  2127.0 107.7 %copy-start.29 = (f32[128,2048]{1,0:T(8,128)S(1)}, f32[128,2048]{1,0:T(8,128)}, u32[]{:S(2)}) copy-start(f32[128,2048]{1,0:T(8,128)} %copy-done.28) | copy-start | bytes 3145732
  2127.0 107.7 %copy-start.38 = (bf16[1,128,2048]{1,2,0:T(8,128)(2,1)S(1)}, bf16[1,128,2048]{1,2,0:T(8,128)(2,1)}, u32[]{:S(2)}) copy-start(bf16[1,128,2048]{1,2,0:T(8,128)(2,1)} %copy-done.37) | copy-start | bytes 1572868
  2127.0 107.7 %copy-start.40 = (bf16[1,128,2048]{1,2,0:T(8,128)(2,1)S(1)}, bf16[1,128,2048]{1,2,0:T(8,128)(2,1)}, u32[]{:S(2)}) copy-start(bf16[1,128,2048]{1,2,0:T(8,128)(2,1)} %copy-done.39) | copy-start | bytes 1572868
  2127.0 107.7 %copy-start.42 = (bf16[1,128,2048]{1,2,0:T(8,128)(2,1)S(1)}, bf16[1,128,2048]{1,2,0:T(8,128)(2,1)}, u32[]{:S(2)}) copy-start(bf16[1,128,2048]{1,2,0:T(8,128)(2,1)} %copy-done.41) | copy-start | bytes 1572868
  2127.0 236.4 %all-reduce.3.cloned.1.call-start = ((), (), s32[]{:S(2)}) async-start(), calls=%async_computation.14 | async-start | bytes 6029312 | tf_op jit(solution)/shard_map/psum | solution.py:368
  (43 other events, 187.2 us)
Sparse Core Ops, SparseCore 0:
  9.5 29.8 all-gather.9
  41.0 201.5 all-gather.7
  244.2 28.4 all-gather.13
  275.2 74.6 all-gather.11
  352.3 72.8 all-gather.17
  426.6 846.1 all-gather.15
  1818.4 147.7 reduce-scatter.4
  1969.8 146.9 reduce-scatter.6
  2119.4 57.0 reduce-scatter.10
  2178.9 54.5 reduce-scatter.8
  2237.2 126.1 all-reduce.2
